TPU v7x, 256 devices: a whole 4x4x8 slice. The times are simulated.
256 devices in a mesh: band: 8 (over z_lo, core), span: 32 (over x, y, z_hi).
Axes of the slice: x: 4, y: 4, z: 8 (z_hi: 2, z_lo: 4; z = z_hi * 4 + z_lo), core: 2. Of those that a mesh axis runs over, the one named last changes fastest.
Arguments:
- gases: bfloat16 [7, 32, 131072], P(None, None, ('band', 'span')), may hold values from 0 to 1
- pressure_bin: int32 [32, 131072], P(None, ('band', 'span')), may hold values from 0 to 59
- layer_mass: bfloat16 [32, 131072], P(None, ('band', 'span')), may hold values from 0.5 to 2
- cos_zenith: bfloat16 [131072], P(('band', 'span')), may hold values from 0.19921875 to 1
- surface_albedo: bfloat16 [131072], P(('band', 'span')), may hold values from 0.049804688 to 0.8984375
- column_order: int32 [131072], P(('band', 'span')), may hold values from 0 to 511, as said below
- sunlit: int32 [1024], P(('band', 'span')), may hold values from 0 to 1, as said below
- absorption: bfloat16 [112, 7, 60], replicated, may hold values from 9.9658966e-05 to 0.099609375
- scattering: bfloat16 [112, 60], replicated, may hold values from 0.19921875 to 0.94921875
Outputs:
- heating: float32 [32, 131072], P(None, ('band', 'span'))
Inputs may be any that keep to these rules, and one draw needn't show every extreme that they name: `column_order`: the 512 entries of each device's slice are a permutation of 0 to 511. The 8 devices with the same index along the second mesh axis hold 16 sunlit blocks together; among them one device has all 4 blocks sunlit and one has none.
All inputs are finite; a program needn't handle non-finite values.
Results may differ from a plain program's by a relative error of at most 0.0003.
Values may be sent and summed in bfloat16 or wider, within the bound.
A program may use at most 64 MiB of HBM per device.

v0:
```python
import jax
import jax.numpy as jnp
from jax import lax
from jax.sharding import PartitionSpec as P


def column_heating(profile, ground_pair, absorption, scattering):
    gas_count = absorption.shape[1]
    bin_count = scattering.shape[1]
    levels = profile.shape[1]
    col_count = profile.shape[2]
    groups = levels // 8
    amounts = profile[:gas_count]
    bin_index = profile[gas_count].astype(jnp.int32)
    thickness = profile[gas_count + 1].astype(jnp.float32)
    cosine = ground_pair[0, 0].astype(jnp.float32)
    ground = ground_pair[1, 0].astype(jnp.float32)
    selector = (
        bin_index[None] == lax.broadcasted_iota(jnp.int32, (bin_count, levels, col_count), 0)
    ).astype(jnp.bfloat16)
    weighted = (amounts[:, None] * selector[None]).reshape(gas_count * bin_count, levels, col_count)
    table = absorption.reshape(absorption.shape[0], gas_count * bin_count)
    optical_depth = jnp.einsum("gk,kln->lgn", table, weighted, preferred_element_type=jnp.float32)
    albedo = jnp.einsum("gk,kln->lgn", scattering, selector, preferred_element_type=jnp.float32)
    column_path = jnp.cumsum(optical_depth, axis=0)
    column_path = jnp.concatenate([jnp.zeros_like(column_path[:1]), column_path], axis=0)
    direct = cosine * jnp.exp(-column_path / cosine)
    fading = jnp.exp(-1.66 * optical_depth)
    reflect = 0.5 * albedo * (1.0 - fading)
    transmit = fading + reflect
    source = 0.5 * albedo * (direct[:-1] - direct[1:])
    grouped_shape = (groups, 8) + reflect.shape[1:]

    def upward(state_pair, layer):
        refl_below, source_below = state_pair
        layer_reflect, layer_transmit, layer_source = layer
        refl_rows = []
        source_rows = []
        for offset in range(7, -1, -1):
            denominator = 1.0 - layer_reflect[offset] * refl_below
            refl_next = (
                layer_reflect[offset]
                + layer_transmit[offset] * layer_transmit[offset] * refl_below / denominator
            )
            source_below = (
                layer_source[offset]
                + layer_transmit[offset]
                * (source_below + refl_below * layer_source[offset])
                / denominator
            )
            refl_below = refl_next
            refl_rows.insert(0, refl_below)
            source_rows.insert(0, source_below)
        return ((refl_below, source_below), (jnp.stack(refl_rows), jnp.stack(source_rows)))

    floor_refl = jnp.broadcast_to(ground, reflect.shape[1:])
    floor_source = ground * direct[-1]
    final_pair, tops = lax.scan(
        upward,
        (floor_refl, floor_source),
        (
            reflect.reshape(grouped_shape),
            transmit.reshape(grouped_shape),
            source.reshape(grouped_shape),
        ),
        reverse=True,
    )
    refl_all = jnp.concatenate([tops[0].reshape(reflect.shape), floor_refl[None]], axis=0)
    source_all = jnp.concatenate([tops[1].reshape(reflect.shape), floor_source[None]], axis=0)

    def downward(diffuse, layer):
        layer_reflect, layer_transmit, layer_source, refl_low, source_low = layer
        level_rows = []
        for offset in range(8):
            denominator = 1.0 - layer_reflect[offset] * refl_low[offset]
            diffuse = (
                layer_transmit[offset] * diffuse
                + layer_reflect[offset] * source_low[offset]
                + layer_source[offset]
            ) / denominator
            level_rows.append(diffuse)
        return (diffuse, jnp.stack(level_rows))

    start_diffuse = jnp.zeros_like(floor_refl)
    final_diffuse, lower = lax.scan(
        downward,
        start_diffuse,
        (
            reflect.reshape(grouped_shape),
            transmit.reshape(grouped_shape),
            source.reshape(grouped_shape),
            refl_all[1:].reshape(grouped_shape),
            source_all[1:].reshape(grouped_shape),
        ),
    )
    diffuse_all = jnp.concatenate([start_diffuse[None], lower.reshape(reflect.shape)], axis=0)
    net = direct + diffuse_all - (refl_all * diffuse_all + source_all)
    return jnp.sum(net[:-1] - net[1:], axis=1) / thickness


def blocks_heating(field_blocks, ground_blocks, absorption, scattering):
    moved_fields = jnp.moveaxis(field_blocks, 2, 0)
    moved_ground = jnp.moveaxis(ground_blocks, 2, 0)
    result = lax.map(
        lambda inputs_pair: column_heating(inputs_pair[0], inputs_pair[1], absorption, scattering),
        (moved_fields, moved_ground),
    )
    return jnp.moveaxis(result, 0, 1)


def local(
    gases,
    pressure_bin,
    layer_mass,
    cos_zenith,
    surface_albedo,
    column_order,
    sunlit,
    absorption,
    scattering,
):
    band_count = lax.axis_size("band")
    group_size = lax.axis_size("span")
    me_band = lax.axis_index("band")
    columns = column_order.shape[0]
    per_peer = columns // group_size
    block_count = sunlit.shape[0]
    block_cols = columns // block_count
    levels = layer_mass.shape[0]
    fields = jnp.concatenate(
        [gases, pressure_bin.astype(jnp.bfloat16)[None], layer_mass[None]], axis=0
    )
    field_rows = fields.shape[0]
    ground = jnp.stack([cos_zenith, surface_albedo])[:, None]
    ordering = column_order.reshape(group_size, per_peer)
    fields = jnp.take(fields, ordering, axis=2)
    ground = jnp.take(ground, ordering, axis=2)
    fields, ground = (
        lax.all_to_all(fields, "span", split_axis=2, concat_axis=2, tiled=True),
        lax.all_to_all(ground, "span", split_axis=2, concat_axis=2, tiled=True),
    )
    fields = fields.reshape(field_rows, levels, block_count, block_cols)
    ground = ground.reshape(2, 1, block_count, block_cols)
    flag_mask = sunlit.astype(jnp.float32)[:, None]
    flag_table = lax.all_gather(sunlit, "band", axis=0, tiled=True).reshape(band_count, block_count)
    counts = jnp.sum(flag_table, axis=1)
    band_ends = jnp.cumsum(counts)
    starts = band_ends - counts
    own_start = starts[me_band]
    own_rank = jnp.cumsum(sunlit) - sunlit
    slot_count = -(-block_count // band_count)
    working = block_count // 2
    target = jnp.arange(band_count, dtype=jnp.int32)[:, None]
    position = jnp.arange(slot_count, dtype=jnp.int32)[None, :]
    wanted = position * band_count + (target - own_start) % band_count
    matches = (sunlit[None, None, :] == 1) & (own_rank[None, None, :] == wanted[:, :, None])
    chosen = jnp.sum(
        jnp.where(matches, jnp.arange(block_count, dtype=jnp.int32), 0), axis=2
    ).reshape(-1)
    send_fields = jnp.take(fields, chosen, axis=2).reshape(
        field_rows, levels, band_count, slot_count, block_cols
    )
    send_ground = jnp.take(ground, chosen, axis=2).reshape(2, 1, band_count, slot_count, block_cols)
    got_fields, got_ground = (
        lax.all_to_all(send_fields, "band", split_axis=2, concat_axis=2, tiled=True),
        lax.all_to_all(send_ground, "band", split_axis=2, concat_axis=2, tiled=True),
    )
    work_rank = jnp.arange(working, dtype=jnp.int32) * band_count + me_band
    source_band = jnp.sum((band_ends[None, :] <= work_rank[:, None]).astype(jnp.int32), axis=1)
    within = work_rank - starts[source_band]
    work_pick = source_band * slot_count + within // band_count
    work_fields = jnp.take(
        got_fields.reshape(field_rows, levels, band_count * slot_count, block_cols),
        work_pick,
        axis=2,
    )
    work_ground = jnp.take(
        got_ground.reshape(2, 1, band_count * slot_count, block_cols), work_pick, axis=2
    )
    heating = blocks_heating(work_fields, work_ground, absorption, scattering)
    inner_back = position * band_count + (me_band - starts[:, None]) % band_count
    rank_back = starts[:, None] + inner_back
    slot_back = jnp.clip(rank_back // band_count, 0, working - 1).reshape(-1)
    returned = jnp.take(heating, slot_back, axis=1).reshape(
        levels, band_count, slot_count, block_cols
    )
    home_heat = lax.all_to_all(returned, "band", split_axis=1, concat_axis=1, tiled=True)
    dest_back = (own_start + own_rank) % band_count
    spot_index = dest_back * slot_count + own_rank // band_count
    physics_heat = (
        jnp.take(home_heat.reshape(levels, band_count * slot_count, block_cols), spot_index, axis=1)
        * flag_mask
    )
    physics_heat = physics_heat.reshape(levels, group_size, per_peer)
    dyn_heat = lax.all_to_all(
        physics_heat, "span", split_axis=1, concat_axis=1, tiled=True
    ).reshape(levels, columns)
    return jnp.zeros((levels, columns), jnp.float32).at[:, column_order].set(dyn_heat)


def solution(mesh):
    placed = (
        P(None, None, ("band", "span")),
        P(None, ("band", "span")),
        P(None, ("band", "span")),
        P(("band", "span")),
        P(("band", "span")),
        P(("band", "span")),
        P(("band", "span")),
        P(),
        P(),
    )
    return jax.shard_map(
        local, mesh=mesh, in_specs=placed, out_specs=P(None, ("band", "span")), check_vma=False
    )
```

profile of v0, /device:TPU:1, one launch (start us, length us, event | category | flops | bytes accessed | tf_op | source)
XLA Modules:
  0.0 282.3 jit_solution(17097676135511918596)
XLA Ops:
  5.5 14.5 %all-to-all-start = ((bf16[2,1,32,16]{3,0,1,2:T(2,128)(2,1)}), bf16[2,1,32,16]{3,0,1,2:T(2,128)(2,1)S(1)}, u32[]{:S(2)}, u32[]{:S(2)}) async-start(bf16[2,1,32,16]{3,0,1,2:T(2,128)(2,1)} %broadcast_select_fusion.1), calls=%async_computation | async-start | bytes 32768 | tf_op jit(solution)/shard_map/all_to_all | solution.py:140
  22.8 6.8 %all-reduce.2 = s32[32]{0:T(128)S(1)} all-reduce(s32[32]{0:T(128)S(1)} %dynamic-update-slice), channel_id=1, replica_groups=mesh['band'=8,'span'=32] {'band'}, use_global_device_ids=true, to_apply=%add.2 | all-reduce | flops 32 | bytes 256
  32.7 1.9 compare_and_fusion.4
  36.5 2.0 copy.76
  38.5 2.7 gather_fusion.4
  41.2 1.9 copy.77
  45.1 11.3 %all-to-all-start.2 = ((bf16[32,2,2304]{2,1,0:T(2,128)(2,1)}), bf16[32,2,2304]{2,1,0:T(2,128)(2,1)S(1)}, u32[]{:S(2)}, u32[]{:S(2)}) async-start(bf16[32,2,2304]{2,1,0:T(2,128)(2,1)} %reshape.960), calls=%async_computation.2 | async-start | bytes 589824 | tf_op jit(solution)/shard_map/all_to_all | solution.py:139
  58.5 10.5 %all-to-all-done.2 = bf16[32,2,2304]{2,1,0:T(2,128)(2,1)S(1)} async-done(((bf16[32,2,2304]{2,1,0:T(2,128)(2,1)}), bf16[32,2,2304]{2,1,0:T(2,128)(2,1)S(1)}, u32[]{:S(2)}, u32[]{:S(2)}) %all-to-all-start.2) | async-done | bytes 294944 | tf_op jit(solution)/shard_map/all_to_all | solution.py:139
  69.0 7.7 %all-to-all-start.1 = ((bf16[2,1,8,1,128]{4,0,3,1,2:T(2,128)(2,1)}), bf16[2,1,8,1,128]{4,0,3,1,2:T(2,128)(2,1)S(1)}, u32[]{:S(2)}, u32[]{:S(2)}) async-start(bf16[2,1,8,1,128]{4,0,3,1,2:T(2,128)(2,1)} %fusion.84), calls=%async_computation.1 | async-start | bytes 8192 | tf_op jit(solution)/shard_map/all_to_all | solution.py:166
  79.6 1.9 all-to-all-done.1
  81.5 4.1 %all-to-all-start.3 = ((bf16[9,32,8,1,128]{4,1,0,3,2:T(8,128)(2,1)}), bf16[9,32,8,1,128]{4,1,0,3,2:T(8,128)(2,1)S(1)}, u32[]{:S(2)}, u32[]{:S(2)}) async-start(bf16[9,32,8,1,128]{4,1,0,3,2:T(8,128)(2,1)} %fusion.81), calls=%async_computation.3 | async-start | bytes 1179648 | tf_op jit(solution)/shard_map/all_to_all | solution.py:165
  86.4 15.1 %all-to-all-done.3 = bf16[9,32,8,1,128]{4,1,0,3,2:T(8,128)(2,1)S(1)} async-done(((bf16[9,32,8,1,128]{4,1,0,3,2:T(8,128)(2,1)}), bf16[9,32,8,1,128]{4,1,0,3,2:T(8,128)(2,1)S(1)}, u32[]{:S(2)}, u32[]{:S(2)}) %all-to-all-start.3) | async-done | bytes 589856 | tf_op jit(solution)/shard_map/all_to_all | solution.py:165
  102.2 148.1 %while.85 = (s32[]{:T(128)}, f32[2,32,128]{2,1,0:T(8,128)S(1)}, bf16[2,2,1,128]{3,0,1,2:T(2,128)(2,1)S(1)}, bf16[2,9,32,128]{3,2,1,0:T(8,128)(2,1)S(1)}, bf16[11...) while((s32[]{:T(128)}, f32[2,32,128]{2,1,0:T(8,128)S(1)}, ...), condition=%wide.region_12.13_spmd, body=%wide.region_5.12_spmd.sunk | while | flops 469948672 | bytes 88375600 | solution.py:104
  103.2 5.9 %fusion.127 = f32[32,112,128]{2,1,0:T(8,128)S(1)} fusion(f32[32,128,112,1]{1,2,3,0:T(8,128)S(1)} %fusion.126), kind=kOutput, calls=%fused_computation.191.clone.1 | output fusion | flops 14221312 | bytes 3670016 | tf_op jit(solution)/shard_map/while/body/eval_jaxpr/jit(cumsum)/reduce_window_sum | solution.py:25
  110.4 2.8 bitcast_multiply_fusion.5
  116.0 14.0 %while.86 = (s32[]{:T(128)}, f32[112,128]{1,0:T(8,128)S(1)}, f32[112,128]{1,0:T(8,128)S(1)}, f32[4,8,112,128]{3,2,1,0:T(8,128)}, f32[4,8,112,128]{3,2,1,0:T(8,12...) while((s32[]{:T(128)}, f32[112,128]{1,0:T(8,128)S(1)}, ...), condition=%wide.region_8.8_spmd, body=%wide.region_7.7_spmd.sunk | while | flops 1290248 | bytes 6136109 | solution.py:58
  130.0 3.5 %fusion.131 = f32[32,112,128]{2,1,0:T(8,128)} fusion(f32[1,112,128]{2,1,0:T(8,128)S(1)} %broadcast_in_dim.228, f32[32,112,128]{2,1,0:T(8,128)} %bitcast.650), kind=kLoop, calls=%fused_computation.184.clone.1 | loop fusion | flops 458752 | bytes 3727360 | tf_op jit(solution)/shard_map/while/body/eval_jaxpr/concatenate | solution.py:68
  134.3 2.9 %fusion.130 = f32[32,112,128]{2,1,0:T(8,128)} fusion(f32[1,112,128]{2,1,0:T(8,128)S(1)} %slice_multiply_fusion.2, f32[32,112,128]{2,1,0:T(8,128)} %bitcast.648), kind=kLoop, calls=%fused_computation.183.clone.1 | loop fusion | flops 458752 | bytes 3727360 | tf_op jit(solution)/shard_map/while/body/eval_jaxpr/concatenate | solution.py:69
  138.5 34.4 %while.87 = (s32[]{:T(128)}, f32[112,128]{1,0:T(8,128)S(1)}, f32[4,8,112,128]{3,2,1,0:T(8,128)}, f32[4,8,112,128]{3,2,1,0:T(8,128)}, f32[4,8,112,128]{3,2,1,0:T(...) while((s32[]{:T(128)}, f32[112,128]{1,0:T(8,128)S(1)}, ...), condition=%wide.region_10.10_spmd.clone, body=%wide.region_9.9_spmd.clone.sunk | while | flops 817161 | bytes 4588343 | solution.py:85
  172.9 3.2 %fusion.132 = f32[33,112,128]{2,1,0:T(8,128)S(1)} fusion(f32[1,112,128]{2,1,0:T(8,128)S(1)} %slice_multiply_fusion.2, f32[1,112,128]{2,1,0:T(8,128)S(1)} %broadcast_in_dim.228, f32[32,112,128]{2,1,0:T(8,128)} %bitcast.684, f32[32,112,128]{2,1,0:T(8,128)} %bitcast.648, f32[32,112,128]{2,1,0:T(8,128)} %bitcast.650, f32[32,112,128]{2,1,0:T(8,128)S(1)} %copy-done.2, ...), kind=kLoop, calls=%fused_computation.180.clone.1 | loop fusion | flops 4257792 | bytes 9347584 | tf_op jit(solution)/shard_map/while/body/eval_jaxpr/sub | solution.py:97
  177.2 5.9 %fusion.127 = f32[32,112,128]{2,1,0:T(8,128)S(1)} fusion(f32[32,128,112,1]{1,2,3,0:T(8,128)S(1)} %fusion.126), kind=kOutput, calls=%fused_computation.191.clone.1 | output fusion | flops 14221312 | bytes 3670016 | tf_op jit(solution)/shard_map/while/body/eval_jaxpr/jit(cumsum)/reduce_window_sum | solution.py:25
  184.4 2.8 bitcast_multiply_fusion.5
  190.0 14.0 %while.86 = (s32[]{:T(128)}, f32[112,128]{1,0:T(8,128)S(1)}, f32[112,128]{1,0:T(8,128)S(1)}, f32[4,8,112,128]{3,2,1,0:T(8,128)}, f32[4,8,112,128]{3,2,1,0:T(8,12...) while((s32[]{:T(128)}, f32[112,128]{1,0:T(8,128)S(1)}, ...), condition=%wide.region_8.8_spmd, body=%wide.region_7.7_spmd.sunk | while | flops 1290248 | bytes 6136109 | solution.py:58
  204.0 3.5 %fusion.131 = f32[32,112,128]{2,1,0:T(8,128)} fusion(f32[1,112,128]{2,1,0:T(8,128)S(1)} %broadcast_in_dim.228, f32[32,112,128]{2,1,0:T(8,128)} %bitcast.650), kind=kLoop, calls=%fused_computation.184.clone.1 | loop fusion | flops 458752 | bytes 3727360 | tf_op jit(solution)/shard_map/while/body/eval_jaxpr/concatenate | solution.py:68
  208.3 2.9 %fusion.130 = f32[32,112,128]{2,1,0:T(8,128)} fusion(f32[1,112,128]{2,1,0:T(8,128)S(1)} %slice_multiply_fusion.2, f32[32,112,128]{2,1,0:T(8,128)} %bitcast.648), kind=kLoop, calls=%fused_computation.183.clone.1 | loop fusion | flops 458752 | bytes 3727360 | tf_op jit(solution)/shard_map/while/body/eval_jaxpr/concatenate | solution.py:69
  212.6 34.4 %while.87 = (s32[]{:T(128)}, f32[112,128]{1,0:T(8,128)S(1)}, f32[4,8,112,128]{3,2,1,0:T(8,128)}, f32[4,8,112,128]{3,2,1,0:T(8,128)}, f32[4,8,112,128]{3,2,1,0:T(...) while((s32[]{:T(128)}, f32[112,128]{1,0:T(8,128)S(1)}, ...), condition=%wide.region_10.10_spmd.clone, body=%wide.region_9.9_spmd.clone.sunk | while | flops 817161 | bytes 4588343 | solution.py:85
  247.0 3.2 %fusion.132 = f32[33,112,128]{2,1,0:T(8,128)S(1)} fusion(f32[1,112,128]{2,1,0:T(8,128)S(1)} %slice_multiply_fusion.2, f32[1,112,128]{2,1,0:T(8,128)S(1)} %broadcast_in_dim.228, f32[32,112,128]{2,1,0:T(8,128)} %bitcast.684, f32[32,112,128]{2,1,0:T(8,128)} %bitcast.648, f32[32,112,128]{2,1,0:T(8,128)} %bitcast.650, f32[32,112,128]{2,1,0:T(8,128)S(1)} %copy-done.2, ...), kind=kLoop, calls=%fused_computation.180.clone.1 | loop fusion | flops 4257792 | bytes 9347584 | tf_op jit(solution)/shard_map/while/body/eval_jaxpr/sub | solution.py:97
  251.6 4.2 %all-to-all-start.4 = ((f32[32,8,1,128]{3,0,2,1:T(8,128)}), f32[32,8,1,128]{3,0,2,1:T(8,128)S(1)}, u32[]{:S(2)}, u32[]{:S(2)}) async-start(f32[32,8,1,128]{3,0,2,1:T(8,128)} %bitcast_select_fusion.1), calls=%async_computation.4 | async-start | bytes 262144 | tf_op jit(solution)/shard_map/all_to_all | solution.py:187
  256.2 5.5 %all-to-all-done.4 = f32[32,8,1,128]{3,0,2,1:T(8,128)S(1)} async-done(((f32[32,8,1,128]{3,0,2,1:T(8,128)}), f32[32,8,1,128]{3,0,2,1:T(8,128)S(1)}, u32[]{:S(2)}, u32[]{:S(2)}) %all-to-all-start.4) | async-done | bytes 131104 | tf_op jit(solution)/shard_map/all_to_all | solution.py:187
  263.3 3.9 %all-to-all-start.5 = ((f32[32,1,512]{2,1,0:T(1,128)}), f32[32,1,512]{2,1,0:T(1,128)S(1)}, u32[]{:S(2)}, u32[]{:S(2)}) async-start(f32[32,1,512]{2,1,0:T(1,128)} %reshape.962), calls=%async_computation.5 | async-start | bytes 131072 | tf_op jit(solution)/shard_map/all_to_all | solution.py:195
  267.2 11.1 %all-to-all-done.5 = f32[32,1,512]{2,1,0:T(1,128)S(1)} async-done(((f32[32,1,512]{2,1,0:T(1,128)}), f32[32,1,512]{2,1,0:T(1,128)S(1)}, u32[]{:S(2)}, u32[]{:S(2)}) %all-to-all-start.5) | async-done | bytes 65568 | tf_op jit(solution)/shard_map/all_to_all | solution.py:195
  279.7 1.8 scatter_custom_fusion
  (349 shorter events, 136.6 us)
Async XLA Ops:
  5.5 39.7 %all-to-all-start = ((bf16[2,1,32,16]{3,0,1,2:T(2,128)(2,1)}), bf16[2,1,32,16]{3,0,1,2:T(2,128)(2,1)S(1)}, u32[]{:S(2)}, u32[]{:S(2)}) async-start(bf16[2,1,32,16]{3,0,1,2:T(2,128)(2,1)} %broadcast_select_fusion.1), calls=%async_computation | async-start | bytes 32768 | tf_op jit(solution)/shard_map/all_to_all | solution.py:140
  45.1 23.9 %all-to-all-start.2 = ((bf16[32,2,2304]{2,1,0:T(2,128)(2,1)}), bf16[32,2,2304]{2,1,0:T(2,128)(2,1)S(1)}, u32[]{:S(2)}, u32[]{:S(2)}) async-start(bf16[32,2,2304]{2,1,0:T(2,128)(2,1)} %reshape.960), calls=%async_computation.2 | async-start | bytes 589824 | tf_op jit(solution)/shard_map/all_to_all | solution.py:139
  69.0 12.5 %all-to-all-start.1 = ((bf16[2,1,8,1,128]{4,0,3,1,2:T(2,128)(2,1)}), bf16[2,1,8,1,128]{4,0,3,1,2:T(2,128)(2,1)S(1)}, u32[]{:S(2)}, u32[]{:S(2)}) async-start(bf16[2,1,8,1,128]{4,0,3,1,2:T(2,128)(2,1)} %fusion.84), calls=%async_computation.1 | async-start | bytes 8192 | tf_op jit(solution)/shard_map/all_to_all | solution.py:166
  78.6 23.6 %copy-start.4 = (bf16[112,60]{0,1:T(8,128)(2,1)S(1)}, bf16[112,60]{0,1:T(8,128)(2,1)}, u32[]{:S(2)}) copy-start(bf16[112,60]{0,1:T(8,128)(2,1)} %param.23) | copy-start | bytes 40324
  78.6 23.6 %copy-start.10 = (bf16[112,7,60]{0,2,1:T(8,128)(2,1)S(1)}, bf16[112,7,60]{0,2,1:T(8,128)(2,1)}, u32[]{:S(2)}) copy-start(bf16[112,7,60]{0,2,1:T(8,128)(2,1)} %param.22) | copy-start | bytes 282244
  81.5 19.9 %all-to-all-start.3 = ((bf16[9,32,8,1,128]{4,1,0,3,2:T(8,128)(2,1)}), bf16[9,32,8,1,128]{4,1,0,3,2:T(8,128)(2,1)S(1)}, u32[]{:S(2)}, u32[]{:S(2)}) async-start(bf16[9,32,8,1,128]{4,1,0,3,2:T(8,128)(2,1)} %fusion.81), calls=%async_computation.3 | async-start | bytes 1179648 | tf_op jit(solution)/shard_map/all_to_all | solution.py:165
  102.2 148.7 %copy-start.6 = (pred[8]{0:T(512)(128)(4,1)S(1)}, pred[8]{0:T(512)(128)(4,1)}, u32[]{:S(2)}) copy-start(pred[8]{0:T(512)(128)(4,1)} %get-tuple-element.492) | copy-start | bytes 28
  102.2 153.7 %copy-start.8 = (s32[4]{0:T(128)S(1)}, s32[4]{0:T(128)}, u32[]{:S(2)}) copy-start(s32[4]{0:T(128)} %param.21) | copy-start | bytes 52
  102.2 153.6 %copy-start.9 = (pred[4]{0:T(512)(128)(4,1)S(1)}, pred[4]{0:T(512)(128)(4,1)}, u32[]{:S(2)}) copy-start(pred[4]{0:T(512)(128)(4,1)} %get-tuple-element.489) | copy-start | bytes 16
  102.2 154.0 %copy-start.7 = (s32[4]{0:T(128)S(1)}, s32[4]{0:T(128)}, u32[]{:S(2)}) copy-start(s32[4]{0:T(128)} %get-tuple-element.490) | copy-start | bytes 52
  109.1 1.2 copy-start.1
  110.4 2.8 copy-start.3
  130.0 3.5 %copy-start = (f32[4,8,112,128]{3,2,1,0:T(8,128)}, f32[4,8,112,128]{3,2,1,0:T(8,128)S(1)}, u32[]{:S(2)}) copy-start(f32[4,8,112,128]{3,2,1,0:T(8,128)S(1)} %get-tuple-element.953) | copy-start | bytes 5505028 | tf_op jit(solution)/shard_map/while
  138.5 34.4 %copy-start.2 = (f32[32,112,128]{2,1,0:T(8,128)S(1)}, f32[32,112,128]{2,1,0:T(8,128)}, u32[]{:S(2)}) copy-start(f32[32,112,128]{2,1,0:T(8,128)} %copy-done.1) | copy-start | bytes 5505028 | tf_op jit(solution)/shard_map/while
  183.2 1.2 copy-start.1
  184.4 2.8 copy-start.3
  204.0 3.5 %copy-start = (f32[4,8,112,128]{3,2,1,0:T(8,128)}, f32[4,8,112,128]{3,2,1,0:T(8,128)S(1)}, u32[]{:S(2)}) copy-start(f32[4,8,112,128]{3,2,1,0:T(8,128)S(1)} %get-tuple-element.953) | copy-start | bytes 5505028 | tf_op jit(solution)/shard_map/while
  212.6 34.4 %copy-start.2 = (f32[32,112,128]{2,1,0:T(8,128)S(1)}, f32[32,112,128]{2,1,0:T(8,128)}, u32[]{:S(2)}) copy-start(f32[32,112,128]{2,1,0:T(8,128)} %copy-done.1) | copy-start | bytes 5505028 | tf_op jit(solution)/shard_map/while
  250.3 16.9 %copy-start.5 = (s32[512]{0:T(512)S(1)}, s32[512]{0:T(512)}, u32[]{:S(2)}) copy-start(s32[512]{0:T(512)} %param.20) | copy-start | bytes 6148
  251.6 10.1 %all-to-all-start.4 = ((f32[32,8,1,128]{3,0,2,1:T(8,128)}), f32[32,8,1,128]{3,0,2,1:T(8,128)S(1)}, u32[]{:S(2)}, u32[]{:S(2)}) async-start(f32[32,8,1,128]{3,0,2,1:T(8,128)} %bitcast_select_fusion.1), calls=%async_computation.4 | async-start | bytes 262144 | tf_op jit(solution)/shard_map/all_to_all | solution.py:187
  263.3 15.0 %all-to-all-start.5 = ((f32[32,1,512]{2,1,0:T(1,128)}), f32[32,1,512]{2,1,0:T(1,128)S(1)}, u32[]{:S(2)}, u32[]{:S(2)}) async-start(f32[32,1,512]{2,1,0:T(1,128)} %reshape.962), calls=%async_computation.5 | async-start | bytes 131072 | tf_op jit(solution)/shard_map/all_to_all | solution.py:195
where the time goes:
time: 288 us; the launch traced here: 282 us
  other arithmetic  125 us (43%)
  local copies, waits for them, and re-layouts  51.3 us (18%)
  starting transfers between devices  45.7 us (16%)
  waiting for transfers between devices  44 us (15%)
  matrix products  7 us (2%)
  blocking collectives  6.82 us (2%)
    while x74, other arithmetic  72.5 us
    all_to_all x1, waiting for transfers between devices, local(): lax.all_to_all(send_fields, 'band', split_axis=2, concat_axis=2, tiled=True)  15.1 us
    dynamic_update_slice x16, local copies, waits for them, and re-layouts, column_heating(): lax.scan(upward, (floor_refl, floor_source), (reflect.reshape(grouped_sha...  14.5 us
    all_to_all x1, starting transfers between devices, local(): lax.all_to_all(ground, 'span', split_axis=2, concat_axis=2, tiled=True)  14.5 us
    another operation x2, other arithmetic, column_heating(): column_path = jnp.cumsum(optical_depth, axis=0)  11.9 us
    all_to_all x1, starting transfers between devices, local(): lax.all_to_all(fields, 'span', split_axis=2, concat_axis=2, tiled=True)  11.3 us
    all_to_all x1, waiting for transfers between devices, local(): lax.all_to_all(physics_heat, 'span', split_axis=1, concat_axis=1, tiled=T...  11.1 us
    all_to_all x1, waiting for transfers between devices, local(): lax.all_to_all(fields, 'span', split_axis=2, concat_axis=2, tiled=True)  10.5 us
  transfers between devices with their start and end apart: 6, of which 5 were waited for; matrix products, arithmetic and copies ran while one was open for 8% of the time, Pallas kernels for 0%

commit v1 on v0

v1 whole, which is shorter than its diff:
```python
import jax, jax.numpy as jnp
from jax import lax
from jax.experimental import pallas as pl
from jax.experimental.pallas import tpu as pltpu
from jax.sharding import PartitionSpec as P
import functools
MESH = pl.DeviceIdType.MESH
F32=jnp.float32; BF16=jnp.bfloat16
LOG2E=1.4426950408889634

INTERP=False
def rowb(ref,c,row,n):
    if INTERP: return jnp.broadcast_to(ref[c,pl.ds(row,1),:],(n,128))
    return ref[c,pl.ds(row,n,stride=0),:]

def body(gas_ref, bin_ref, mass_ref, cos_ref, alb_ref, order_ref, sun_ref, abs_ref, sca_ref, out_ref,
         gas32, bin32, tab32, lhs, tau_s, h_s, ti_s, v_s, p_s, acc, st32, recv, jcol, loc_sem, ssem, rsem):
    me = lax.axis_index("span")
    q = me // 2
    zh = lax.rem(me, 2)
    def peer(d): return {"span": lax.rem(q + d, 16) * 2 + zh}
    def row(d): return zh * 16 + lax.rem(q + d, 16)
    across = {"span": q * 2 + 1 - zh}
    barrier = pltpu.get_barrier_semaphore()
    for d in range(1, 16):
        pl.semaphore_signal(barrier, inc=1, device_id=peer(d), device_id_type=MESH)
    pl.semaphore_signal(barrier, inc=1, device_id=across, device_id_type=MESH)
    own = pltpu.make_async_copy(sun_ref, recv.at[row(0)], loc_sem)
    own.start()
    def flat(d, r):
        return pltpu.make_async_remote_copy(src_ref=sun_ref, dst_ref=recv.at[r], send_sem=ssem.at[d], recv_sem=rsem.at[d],
            device_id=peer(d), device_id_type=MESH)
    def deep(z):
        return pltpu.make_async_remote_copy(src_ref=recv.at[pl.ds(zh * 16, 16)], dst_ref=recv.at[pl.ds(z * 16, 16)],
            send_sem=ssem.at[0], recv_sem=rsem.at[0], device_id=across, device_id_type=MESH)
    trow = lax.broadcasted_iota(jnp.int32, (8, 512), 1)
    trow = (lax.rem(trow // 16, 2) * 16 + trow // 32).astype(F32).astype(BF16)
    order = order_ref[...].reshape(1, 512)
    for c in range(4):
        hot = (lax.broadcasted_iota(jnp.int32, (128, 512), 0) + c * 128 == order).astype(F32).astype(BF16)
        jcol[:, c*128:c*128+128] = lax.dot_general(trow, hot, (((1,), (1,)), ((), ())), preferred_element_type=F32)
    for c in range(4):
        gas32[c] = gas_ref[:,:,c*128:c*128+128].reshape(7*32,128).astype(F32)
        bin32[c] = bin_ref[:,c*128:c*128+128].astype(F32)
    tab32[...] = jnp.zeros_like(tab32)
    for a in range(7):
        tab32[a*64:a*64+60, :112] = abs_ref[a].astype(F32)
    tab32[448:508, :112] = sca_ref[...].astype(F32)*0.5
    lhs[...] = jnp.transpose(tab32[...])[:112].astype(BF16)
    kk = lax.broadcasted_iota(jnp.int32,(64,256),0).astype(F32).astype(BF16)

    @pl.loop(0,32)
    def _(l):
        for g in range(2):
            cs = pl.ds(g*256,256)
            def bc(ref,row):
                return jnp.concatenate([rowb(ref,2*g+q,row,16) for q in range(2)],axis=1).astype(BF16)
            kb = bc(bin32,l)
            kb = jnp.concatenate([kb]*4,axis=0)
            m = (kb==kk)
            ws=[]
            for a in range(7):
                ab = bc(gas32,a*32+l)
                ab = jnp.concatenate([ab]*4,axis=0)
                ws.append(jnp.where(m,ab,jnp.zeros_like(ab)))
            sel = jnp.where(m,jnp.ones_like(ab),jnp.zeros_like(ab))
            W = jnp.concatenate(ws,axis=0)
            tau_s[l,:,cs] = jnp.dot(lhs[:, :448], W, preferred_element_type=F32)
            h_s[l,:,cs] = jnp.dot(lhs[:, 448:], sel, preferred_element_type=F32)

    pl.semaphore_wait(barrier, 16)
    for d in range(1, 16):
        flat(d, row(0)).start()

    mu = cos_ref[...].astype(F32).reshape(1,512)
    al = alb_ref[...].astype(F32).reshape(1,512)
    mb=-LOG2E/mu
    for c in range(4):
        st32[c,0:1,:]=mb[:,c*128:c*128+128]
        st32[c,1:2,:]=al[:,c*128:c*128+128]
    acc[...] = jnp.zeros_like(acc)
    NT=7
    for c in range(4):
        if c == 2:
            own.wait()
            for d in range(1, 16):
                flat(d, row(0)).wait_send()
                flat(d, row(16 - d)).wait_recv()
            deep(zh).start()
        cs = pl.ds(c*128,128)
        cmu = rowb(st32,c,0,8)
        alb = rowb(st32,c,1,8)
        for hf in range(2):
            def gs(i): return pl.ds((hf*NT+i)*8,8)
            zero = jnp.zeros((8,128),F32); one=jnp.ones((8,128),F32)
            def down(l,carry):
                cum,T,Pp,Q = carry
                ncum=[];nT=[];nP=[];nQ=[]
                x = None
                for i in range(NT):
                    tau = tau_s[l,gs(i),cs]; h = h_s[l,gs(i),cs]
                    c1 = cum[i]+tau
                    T1 = jnp.exp2(c1*cmu)
                    f = jnp.exp2(tau*(-1.66*LOG2E))
                    r = h*(1.0-f)
                    t = f+r
                    s = h*(T[i]-T1)
                    den = 1.0-r*Pp[i]
                    y = pl.reciprocal(den,approx=True)
                    inv = y*(2.0-den*y)
                    ti = t*inv
                    v = (r*Q[i]+s)*inv
                    a = ti*Pp[i]
                    b = Pp[i]*v+Q[i]
                    ti_s[l,gs(i),cs]=ti
                    v_s[l,gs(i),cs]=v
                    p_s[l,gs(i),cs]=a-ti
                    xx = T[i]+(b-v)
                    x = xx if x is None else x+xx
                    ncum.append(c1);nT.append(T1);nP.append(r+t*a);nQ.append(s+t*b)
                acc[l,:,cs] = acc[l,:,cs]+x
                return (tuple(ncum),tuple(nT),tuple(nP),tuple(nQ))
            z=(zero,)*NT
            cum,T,Pp,Q = lax.fori_loop(0,32,down,(z,(one,)*NT,z,z))
            U=[]; x=None
            for i in range(NT):
                u = alb*(Q[i]+T[i])/(1.0-alb*Pp[i])
                d = Pp[i]*u+Q[i]
                xx = T[i]+d-u
                x = xx if x is None else x+xx
                U.append(u)
            acc[32,:,cs] = acc[32,:,cs]+x
            def up(k,U):
                l = 31-k
                x=None; nU=[]
                for i in range(NT):
                    xx = p_s[l,gs(i),cs]*U[i]
                    nU.append(ti_s[l,gs(i),cs]*U[i]+v_s[l,gs(i),cs])
                    x = xx if x is None else x+xx
                acc[l,:,cs] = acc[l,:,cs]+x
                return tuple(nU)
            lax.fori_loop(0,32,up,tuple(U))
    deep(zh).wait_send()
    deep(1 - zh).wait_recv()
    flags = recv[...].reshape(32, 4)
    mine = lax.broadcasted_iota(jnp.int32, (32, 4), 1) == me // 8
    flag = jnp.sum(jnp.where(mine, flags, 0).astype(F32), axis=1, keepdims=True)
    j = lax.broadcasted_iota(jnp.int32, (32, 512), 0).astype(F32)
    lit = jnp.sum(jnp.where(jnp.broadcast_to(jcol[0:1, :], (32, 512)) == j, jnp.broadcast_to(flag, (32, 512)), 0.0), axis=0, keepdims=True)
    tot = jnp.sum(acc[...],axis=1)
    out_ref[...] = (tot[:32]-tot[1:])*(lit*mu/mass_ref[...].astype(F32))

def call(*args):
    args=list(args); args[7]=jnp.transpose(args[7],(1,2,0)); args[8]=jnp.transpose(args[8]); args[6]=args[6].reshape(1,4)
    vm = pl.BlockSpec(memory_space=pltpu.VMEM)
    return pl.pallas_call(body, out_shape=jax.ShapeDtypeStruct((32,512),F32),
        in_specs=[vm]*9, out_specs=vm,
        scratch_shapes=[pltpu.VMEM((4,224,128),F32),pltpu.VMEM((4,32,128),F32),pltpu.VMEM((512,128),F32),pltpu.VMEM((112,512),BF16)]
          +[pltpu.VMEM((32,112,512),F32)]*5+[pltpu.VMEM((33,8,512),F32),pltpu.VMEM((4,8,128),F32),
          pltpu.VMEM((32,1,4),jnp.int32),pltpu.VMEM((8,512),F32),pltpu.SemaphoreType.DMA,pltpu.SemaphoreType.DMA((16,)),pltpu.SemaphoreType.DMA((16,))],
        compiler_params=pltpu.CompilerParams(vmem_limit_bytes=60*1024*1024, collective_id=0, has_side_effects=True),
        )(*args)

def solution(mesh):
    s1=P(("band","span"))
    placed=(P(None,None,("band","span")),P(None,("band","span")),P(None,("band","span")),s1,s1,s1,s1,P(),P())
    return jax.shard_map(call,mesh=mesh,in_specs=placed,out_specs=P(None,("band","span")),check_vma=False)
```

time: 288 us -> 30.4 us (0.11)
  the two profiles are of different devices: /device:TPU:1 before, /device:TPU:6 now
where the time goes in v1:
time: 30.4 us; the launch traced here: 30.2 us
  Pallas kernels  28.7 us (94%)
  local copies, waits for them, and re-layouts  1.47 us (5%)
    pallas_call x1, Pallas kernels, call(): pl.pallas_call(body, out_shape=jax.ShapeDtypeStruct((32, 512), F32), in_s...  28.7 us
    unnamed x1, local copies, waits for them, and re-layouts  1.47 us

profile of v1, /device:TPU:6, one launch (start us, length us, event | category | flops | bytes accessed | tf_op | source)
XLA Modules:
  0.0 30.2 jit_solution(11984539700897447607)
XLA Ops:
  0.0 28.7 %shard_map.91 = f32[32,512]{1,0:T(8,128)} custom-call(bf16[7,32,512]{2,1,0:T(8,128)(2,1)} %gas_ref.1, s32[32,512]{1,0:T(8,128)} %bin_ref.1, bf16[32,512]{1,0:T(8,128)(2,1)} %mass_ref.1, bf16[512]{0:T(512)(128)(2,1)} %cos_ref.1, bf16[512]{0:T(512)(128)(2,1)} %alb_ref.1, s32[512]{0:T(512)} %order_ref.1, s32[1,4]{1,0:T(1,128)} %bitcast.5, ...), custom_call_target="tpu_custom_call" | custom-call | tf_op jit(solution)/shard_map/pallas_call | solution.py:156
  28.7 1.5 %copy.11 = f32[32,512]{1,0:T(8,128)} copy(f32[32,512]{1,0:T(8,128)} %shard_map.91) | data formatting | bytes 131072

commit v2 on v1

v2 whole, which is shorter than its diff:
```python
import jax
import jax.numpy as jnp
from jax import lax
from jax.experimental import pallas as pl
from jax.experimental.pallas import tpu as pltpu
from jax.sharding import PartitionSpec as P

MESH = pl.DeviceIdType.MESH
F32 = jnp.float32
BF16 = jnp.bfloat16
LOG2E = 1.4426950408889634
FADE = -1.66 * LOG2E
LANES = 128
GAS = 7
L = 32
G = 112
C = 512
TILES = G // 8
INTERP = False


def wide_row(ref, c, row, n):
    if INTERP:
        return jnp.broadcast_to(ref[c, pl.ds(row, 1), :], (n, LANES))
    return ref[c, pl.ds(row, n, stride=0), :]


def cols(c):
    return slice(c * LANES, (c + 1) * LANES)


def rows(i):
    return slice(i * 8, (i + 1) * 8)


def body(gas_hbm, bin_hbm, mass_hbm, cos_hbm, alb_hbm, order_hbm, sun_ref, abs_hbm, sca_hbm, out_ref,
         gas_ref, bin_ref, mass_ref, cos_ref, alb_ref, order_ref, abs_ref, sca_ref,
         gas32, bin32, tab32, lhs, tau_a, tau_b, h_a, h_b, st_t, st_p, st_q, ti_s, v_s, p_s, acc, per_col,
         heat, recv, jcol, loc_sem, ssem, rsem):
    me = lax.axis_index("span")
    x = me // 8
    y = lax.rem(me // 2, 4)
    zh = lax.rem(me, 2)
    zl = lax.axis_index("band") // 2
    hops = jnp.minimum(x, 2) + jnp.minimum(y, 2)
    moment = jnp.where(zh == 0, (36 - 5 * hops) // 2, jnp.maximum((11 + 3 * zl - 3 * hops) // 2, 0))
    barrier = pltpu.get_barrier_semaphore()

    def turn(d):
        return lax.rem(me + d, 32)

    for d in range(1, 32):
        pl.semaphore_signal(barrier, inc=1, device_id={"span": turn(d)}, device_id_type=MESH)

    loads = [pltpu.make_async_copy(src, dst, loc_sem.at[n]) for n, (src, dst) in enumerate((
        (abs_hbm, abs_ref), (sca_hbm, sca_ref), (gas_hbm, gas_ref), (bin_hbm, bin_ref), (cos_hbm, cos_ref),
        (alb_hbm, alb_ref), (order_hbm, order_ref), (mass_hbm, mass_ref), (sun_ref, recv.at[me])))]
    for v in loads:
        v.start()

    def flag_copy(r, d):
        return pltpu.make_async_remote_copy(
            src_ref=sun_ref, dst_ref=recv.at[r], send_sem=ssem.at[d], recv_sem=rsem.at[d],
            device_id={"span": turn(d)}, device_id_type=MESH)

    def send(when):
        @pl.when(when)
        def _():
            pl.semaphore_wait(barrier, 31)
            for d in range(1, 32):
                flag_copy(me, d).start()

    send(moment == 0)
    for v in loads:
        v.wait()

    for c in range(4):
        gas32[c] = gas_ref[:, :, cols(c)].reshape(GAS * L, LANES).astype(F32)
        bin32[c] = bin_ref[:, cols(c)].astype(F32)
    tab32[...] = jnp.zeros_like(tab32)
    for a in range(GAS):
        tab32[a * 64:a * 64 + 60, :G] = abs_ref[a].astype(F32)
    tab32[448:508, :G] = sca_ref[...].astype(F32) * 0.5
    lhs[...] = jnp.transpose(tab32[...])[:G].astype(BF16)
    kk = lax.broadcasted_iota(jnp.int32, (64, 256), 0).astype(F32).astype(BF16)

    def optics(l, tau_ref, h_ref):
        for g in range(2):
            def spread(ref, r):
                x = jnp.concatenate([wide_row(ref, 2 * g + k, r, 16) for k in range(2)], axis=1).astype(BF16)
                return jnp.concatenate([x] * 4, axis=0)

            here = spread(bin32, l) == kk
            zero = jnp.zeros((64, 256), BF16)
            w = jnp.concatenate([jnp.where(here, spread(gas32, a * L + l), zero) for a in range(GAS)], axis=0)
            sel = jnp.where(here, jnp.ones_like(zero), zero)
            cs = slice(g * 256, g * 256 + 256)
            tau_ref[:, cs] = jnp.dot(lhs[:, :448], w, preferred_element_type=F32)
            h_ref[:, cs] = jnp.dot(lhs[:, 448:], sel, preferred_element_type=F32)

    optics(0, tau_a, h_a)
    mu = cos_ref[...].astype(F32).reshape(1, C)
    rate = -LOG2E / mu
    alb = alb_ref[...].astype(F32).reshape(1, C)
    for c in range(4):
        per_col[c, 0:1, :] = rate[:, cols(c)]
        per_col[c, 1:2, :] = alb[:, cols(c)]
    st_t[...] = jnp.ones_like(st_t)
    st_p[...] = jnp.zeros_like(st_p)
    st_q[...] = jnp.zeros_like(st_q)

    def layer(l, tau_ref, h_ref):
        for c in range(4):
            cs = cols(c)
            rate = wide_row(per_col, c, 0, 8)
            x = None
            for i in range(TILES):
                gs = rows(i)
                tau = tau_ref[gs, cs]
                h = h_ref[gs, cs]
                t0 = st_t[gs, cs]
                p0 = st_p[gs, cs]
                q0 = st_q[gs, cs]
                t1 = t0 * jnp.exp2(tau * rate)
                f = jnp.exp2(tau * FADE)
                r = h * (1.0 - f)
                t = f + r
                s = h * (t0 - t1)
                inv = pl.reciprocal(1.0 - r * p0, approx=False)
                ti = t * inv
                y = q0 + p0 * s
                st_t[gs, cs] = t1
                st_p[gs, cs] = r + t * (ti * p0)
                st_q[gs, cs] = s + ti * y
                ti_s[l, gs, cs] = ti
                v_s[l, gs, cs] = inv * (r * q0 + s)
                p_s[l, gs, cs] = p0
                x = t0 + q0 if x is None else x + (t0 + q0)
            acc[l, :, cs] = x

    def pair(k, carry):
        l = 2 * k
        send((k > 0) & (k == moment))
        optics(l + 1, tau_b, h_b)
        layer(l, tau_a, h_a)
        optics(jnp.minimum(l + 2, L - 1), tau_a, h_a)
        layer(l + 1, tau_b, h_b)
        return carry

    lax.fori_loop(0, L // 2, pair, 0)

    trow = lax.broadcasted_iota(jnp.int32, (8, C), 1)
    trow = (trow // 16).astype(F32).astype(BF16)
    order = order_ref[...].reshape(1, C)
    for c in range(4):
        hot = (lax.broadcasted_iota(jnp.int32, (LANES, C), 0) + c * LANES == order).astype(F32).astype(BF16)
        jcol[:, cols(c)] = lax.dot_general(trow, hot, (((1,), (1,)), ((), ())), preferred_element_type=F32)

    for half in range(2):
        where = [(rows(i), cols(c)) for c in (2 * half, 2 * half + 1) for i in range(TILES)]
        up0 = []
        sums = []
        for n, (gs, cs) in enumerate(where):
            al = wide_row(per_col, 2 * half + n // TILES, 1, 8)
            tt = st_t[gs, cs]
            pp = st_p[gs, cs]
            qq = st_q[gs, cs]
            u = al * (qq + tt) / (1.0 - al * pp)
            up0.append(u)
            sums.append(tt + (pp * u + qq) - u)
        for j in range(2):
            acc[L, :, cols(2 * half + j)] = sum(sums[j * TILES + 1:(j + 1) * TILES], sums[j * TILES])

        def up(k, u):
            for l in (L - 1 - 2 * k, L - 2 - 2 * k):
                u = [ti_s[l, gs, cs] * u[n] + v_s[l, gs, cs] for n, (gs, cs) in enumerate(where)]
                d = [p_s[l, gs, cs] * u[n] - u[n] for n, (gs, cs) in enumerate(where)]
                for j in range(2):
                    cs = cols(2 * half + j)
                    acc[l, :, cs] = acc[l, :, cs] + sum(d[j * TILES + 1:(j + 1) * TILES], d[j * TILES])
            return tuple(u)

        lax.fori_loop(0, L // 2, up, tuple(up0))
        if half == 0:
            send(moment >= L // 2)

    net = jnp.sum(acc[...], axis=1)
    heat[...] = (net[:L] - net[1:]) * (mu / mass_ref[...].astype(F32))
    for d in range(1, 32):
        flag_copy(turn(32 - d), d).wait_recv()
    flags = recv[...].reshape(32, 4)
    mine = lax.broadcasted_iota(jnp.int32, (32, 4), 1) == me // 8
    flag = jnp.sum(jnp.where(mine, flags, 0).astype(F32), axis=1, keepdims=True)
    j = lax.broadcasted_iota(jnp.int32, (32, C), 0).astype(F32)
    lit = jnp.sum(jnp.where(jnp.broadcast_to(jcol[0:1, :], (32, C)) == j, jnp.broadcast_to(flag, (32, C)), 0.0),
                  axis=0, keepdims=True)
    out_ref[...] = heat[...] * lit

    for d in range(1, 32):
        flag_copy(me, d).wait_send()


def local(gases, pressure_bin, layer_mass, cos_zenith, surface_albedo, column_order, sunlit, absorption, scattering):
    vm = pl.BlockSpec(memory_space=pltpu.VMEM)
    state = [pltpu.VMEM((G, C), F32)]
    return pl.pallas_call(
        body,
        out_shape=pltpu.VMEM((L, C), F32),
        in_specs=[pl.BlockSpec(memory_space=pl.ANY)] * 9,
        out_specs=vm,
        scratch_shapes=[
            pltpu.VMEM((GAS, L, C), BF16), pltpu.VMEM((L, C), jnp.int32), pltpu.VMEM((L, C), BF16),
            pltpu.VMEM((C,), BF16), pltpu.VMEM((C,), BF16), pltpu.VMEM((C,), jnp.int32),
            pltpu.VMEM((GAS, 60, G), BF16), pltpu.VMEM((60, G), BF16),
            pltpu.VMEM((4, GAS * L, LANES), F32), pltpu.VMEM((4, L, LANES), F32), pltpu.VMEM((C, LANES), F32),
            pltpu.VMEM((G, C), BF16)] + state * 7 + [pltpu.VMEM((L, G, C), F32)] * 3 + [
            pltpu.VMEM((L + 1, 8, C), F32), pltpu.VMEM((4, 8, LANES), F32),
            pltpu.VMEM((L, C), F32), pltpu.VMEM((32, 1, 4), jnp.int32), pltpu.VMEM((8, C), F32),
            pltpu.SemaphoreType.DMA((9,)), pltpu.SemaphoreType.DMA((32,)), pltpu.SemaphoreType.DMA((32,))],
        compiler_params=pltpu.CompilerParams(
            vmem_limit_bytes=60 * 1024 * 1024, collective_id=0, has_side_effects=True),
    )(gases, pressure_bin, layer_mass, cos_zenith, surface_albedo, column_order, sunlit.reshape(1, 4),
      jnp.transpose(absorption, (1, 2, 0)), jnp.transpose(scattering))


def solution(mesh):
    one = P(("band", "span"))
    two = P(None, ("band", "span"))
    return jax.shard_map(
        local, mesh=mesh, in_specs=(P(None, None, ("band", "span")), two, two, one, one, one, one, P(), P()),
        out_specs=two, check_vma=False)
```

time: 30.4 us -> 19.2 us (0.63)
  Pallas kernels: 28.7 us -> 18.4 us
  local copies, waits for them, and re-layouts: 1.47 us -> 0.63 us
    pallas_call x1, Pallas kernels: 28.7 us -> 18.4 us  [local(): pl.pallas_call(body, out_shape=pltpu.VMEM((L, C), F32), in_specs=[pl.Bloc...]
    unnamed x1, local copies, waits for them, and re-layouts: 1.47 us -> 0.63 us
where the time goes in v2:
time: 19.2 us; the launch traced here: 19.1 us
  Pallas kernels  18.4 us (96%)
  local copies, waits for them, and re-layouts  0.63 us (3%)
    pallas_call x1, Pallas kernels, local(): pl.pallas_call(body, out_shape=pltpu.VMEM((L, C), F32), in_specs=[pl.Bloc...  18.4 us
    unnamed x1, local copies, waits for them, and re-layouts  0.63 us

profile of v2, /device:TPU:6, one launch (start us, length us, event | category | flops | bytes accessed | tf_op | source)
XLA Modules:
  0.0 19.1 jit_solution(3229500128112979278)
XLA Ops:
  0.0 18.4 %shard_map.91 = f32[32,512]{1,0:T(8,128)S(1)} custom-call(bf16[7,32,512]{2,1,0:T(8,128)(2,1)} %gas_hbm.1, s32[32,512]{1,0:T(8,128)} %bin_hbm.1, bf16[32,512]{1,0:T(8,128)(2,1)} %mass_hbm.1, bf16[512]{0:T(512)(128)(2,1)} %cos_hbm.1, bf16[512]{0:T(512)(128)(2,1)} %alb_hbm.1, s32[512]{0:T(512)} %order_hbm.1, s32[1,4]{1,0:T(1,128)} %bitcast.5, ...), custom_call_target="tpu_custom_call" | custom-call | tf_op jit(solution)/shard_map/pallas_call | solution.py:206
  18.4 0.6 %copy.11 = f32[32,512]{1,0:T(8,128)} copy(f32[32,512]{1,0:T(8,128)S(1)} %shard_map.91) | data formatting | bytes 131072

commit v3 on v2

--- a/solution.py
+++ b/solution.py
@@ -38,37 +38,95 @@
          gas32, bin32, tab32, lhs, tau_a, tau_b, h_a, h_b, st_t, st_p, st_q, ti_s, v_s, p_s, acc, per_col,
          heat, recv, jcol, loc_sem, ssem, rsem):
     me = lax.axis_index("span")
-    x = me // 8
-    y = lax.rem(me // 2, 4)
+    q = me // 2
     zh = lax.rem(me, 2)
+    x = q // 4
+    y = lax.rem(q, 4)
     zl = lax.axis_index("band") // 2
     hops = jnp.minimum(x, 2) + jnp.minimum(y, 2)
-    moment = jnp.where(zh == 0, (36 - 5 * hops) // 2, jnp.maximum((11 + 3 * zl - 3 * hops) // 2, 0))
+    direct = zl >= 2
+    first = zh == 0
+    own_row = first | direct
+    mine = zh * 16 + q
+    moment = jnp.where(direct, jnp.where(first, 35 - 3 * zl - 3 * hops, 9 + 3 * zl - 3 * hops),
+                       jnp.where(first, 24 - 3 * hops, jnp.maximum(6 + 3 * zl - 3 * hops, 0))) // 2
+    expected = jnp.where(direct, 31, jnp.where(first, 15, 16))
     barrier = pltpu.get_barrier_semaphore()
 
     def turn(d):
-        return lax.rem(me + d, 32)
-
-    for d in range(1, 32):
-        pl.semaphore_signal(barrier, inc=1, device_id={"span": turn(d)}, device_id_type=MESH)
+        return lax.rem(q + d, 16)
+
+    def device(plane, d):
+        return {"span": turn(d) * 2 + plane}
+
+    def each(plane, act):
+        for d in range(16):
+            if d:
+                act(plane, d)
+            else:
+                pl.when(zh != plane)(lambda: act(plane, 0))
+
+    def signal(plane, d):
+        pl.semaphore_signal(barrier, inc=1, device_id=device(plane, d), device_id_type=MESH)
+
+    @pl.when(own_row)
+    def _():
+        each(1, signal)
+        each(0, signal)
 
     loads = [pltpu.make_async_copy(src, dst, loc_sem.at[n]) for n, (src, dst) in enumerate((
         (abs_hbm, abs_ref), (sca_hbm, sca_ref), (gas_hbm, gas_ref), (bin_hbm, bin_ref), (cos_hbm, cos_ref),
-        (alb_hbm, alb_ref), (order_hbm, order_ref), (mass_hbm, mass_ref), (sun_ref, recv.at[me])))]
+        (alb_hbm, alb_ref), (order_hbm, order_ref), (mass_hbm, mass_ref)))]
+    own = pltpu.make_async_copy(sun_ref, recv.at[mine], loc_sem.at[8])
     for v in loads:
         v.start()
-
-    def flag_copy(r, d):
+    pl.when(own_row)(lambda: own.start())
+
+    def flag_copy(r, plane, d):
         return pltpu.make_async_remote_copy(
-            src_ref=sun_ref, dst_ref=recv.at[r], send_sem=ssem.at[d], recv_sem=rsem.at[d],
-            device_id={"span": turn(d)}, device_id_type=MESH)
+            src_ref=sun_ref, dst_ref=recv.at[r], send_sem=ssem.at[plane * 16 + d], recv_sem=rsem.at[r],
+            device_id=device(plane, d), device_id_type=MESH)
+
+    def table_copy():
+        return pltpu.make_async_remote_copy(
+            src_ref=recv, dst_ref=recv, send_sem=ssem.at[32], recv_sem=rsem.at[32],
+            device_id={"span": q * 2 + 1 - zh}, device_id_type=MESH)
+
+    def start_copy(plane, d):
+        flag_copy(mine, plane, d).start()
+
+    def end_copy(plane, d):
+        flag_copy(mine, plane, d).wait_send()
+
+    def take_row(plane, d):
+        flag_copy(plane * 16 + turn(d), plane, d).wait_recv()
 
     def send(when):
         @pl.when(when)
         def _():
-            pl.semaphore_wait(barrier, 31)
-            for d in range(1, 32):
-                flag_copy(me, d).start()
+            pl.semaphore_wait(barrier, expected)
+            each(0, start_copy)
+            pl.when(direct)(lambda: each(1, start_copy))
+
+    def take_rows(when):
+        @pl.when(when)
+        def _():
+            own.wait()
+            each(0, take_row)
+            each(1, take_row)
+
+    def hand_over():
+        take_rows(first & jnp.logical_not(direct))
+        pl.when(first & jnp.logical_not(direct))(lambda: table_copy().start())
+
+    def finish_rows():
+        take_rows(direct)
+        pl.when(jnp.logical_not(own_row))(lambda: table_copy().wait_recv())
+
+    def end_copies():
+        each(0, end_copy)
+        pl.when(direct)(lambda: each(1, end_copy))
+        pl.when(first & jnp.logical_not(direct))(lambda: table_copy().wait_send())
 
     send(moment == 0)
     for v in loads:
@@ -84,10 +142,14 @@
     lhs[...] = jnp.transpose(tab32[...])[:G].astype(BF16)
     kk = lax.broadcasted_iota(jnp.int32, (64, 256), 0).astype(F32).astype(BF16)
 
-    def optics(l, tau_ref, h_ref):
-        for g in range(2):
+    def optics(l, tau_ref, h_ref, groups=(0, 1), after=None):
+        for g in groups:
             def spread(ref, r):
-                x = jnp.concatenate([wide_row(ref, 2 * g + k, r, 16) for k in range(2)], axis=1).astype(BF16)
+                x = jnp.concatenate([wide_row(ref, 2 * g + k, r, 16) for k in range(2)], axis=1)
+                if ref is bin32 and after is not None:
+                    z = jnp.concatenate([after * 0.0] * 2, axis=0)
+                    x = x + jnp.concatenate([z, z], axis=1)
+                x = x.astype(BF16)
                 return jnp.concatenate([x] * 4, axis=0)
 
             here = spread(bin32, l) == kk
@@ -109,8 +171,9 @@
     st_p[...] = jnp.zeros_like(st_p)
     st_q[...] = jnp.zeros_like(st_q)
 
-    def layer(l, tau_ref, h_ref):
-        for c in range(4):
+    def layer(l, tau_ref, h_ref, tiles):
+        seen = []
+        for c in tiles:
             cs = cols(c)
             rate = wide_row(per_col, c, 0, 8)
             x = None
@@ -137,20 +200,27 @@
                 p_s[l, gs, cs] = p0
                 x = t0 + q0 if x is None else x + (t0 + q0)
             acc[l, :, cs] = x
+            seen.append(x)
+        return seen
 
     def pair(k, carry):
         l = 2 * k
         send((k > 0) & (k == moment))
-        optics(l + 1, tau_b, h_b)
-        layer(l, tau_a, h_a)
-        optics(jnp.minimum(l + 2, L - 1), tau_a, h_a)
-        layer(l + 1, tau_b, h_b)
+        n = jnp.minimum(l + 2, L - 1)
+        x = layer(l, tau_a, h_a, (0, 1))
+        optics(l + 1, tau_b, h_b, (0,))
+        optics(l + 1, tau_b, h_b, (1,), x[0])
+        y = layer(l, tau_a, h_a, (2, 3))
+        x = layer(l + 1, tau_b, h_b, (0, 1))
+        optics(n, tau_a, h_a, (0,), y[1])
+        optics(n, tau_a, h_a, (1,), x[0])
+        layer(l + 1, tau_b, h_b, (2, 3))
         return carry
 
     lax.fori_loop(0, L // 2, pair, 0)
 
     trow = lax.broadcasted_iota(jnp.int32, (8, C), 1)
-    trow = (trow // 16).astype(F32).astype(BF16)
+    trow = (lax.rem(trow // 16, 2) * 16 + trow // 32).astype(F32).astype(BF16)
     order = order_ref[...].reshape(1, C)
     for c in range(4):
         hot = (lax.broadcasted_iota(jnp.int32, (LANES, C), 0) + c * LANES == order).astype(F32).astype(BF16)
@@ -181,23 +251,20 @@
             return tuple(u)
 
         lax.fori_loop(0, L // 2, up, tuple(up0))
-        if half == 0:
-            send(moment >= L // 2)
-
+
+    hand_over()
     net = jnp.sum(acc[...], axis=1)
     heat[...] = (net[:L] - net[1:]) * (mu / mass_ref[...].astype(F32))
-    for d in range(1, 32):
-        flag_copy(turn(32 - d), d).wait_recv()
+    finish_rows()
     flags = recv[...].reshape(32, 4)
-    mine = lax.broadcasted_iota(jnp.int32, (32, 4), 1) == me // 8
-    flag = jnp.sum(jnp.where(mine, flags, 0).astype(F32), axis=1, keepdims=True)
+    block = lax.broadcasted_iota(jnp.int32, (32, 4), 1) == me // 8
+    flag = jnp.sum(jnp.where(block, flags, 0).astype(F32), axis=1, keepdims=True)
     j = lax.broadcasted_iota(jnp.int32, (32, C), 0).astype(F32)
     lit = jnp.sum(jnp.where(jnp.broadcast_to(jcol[0:1, :], (32, C)) == j, jnp.broadcast_to(flag, (32, C)), 0.0),
                   axis=0, keepdims=True)
     out_ref[...] = heat[...] * lit
 
-    for d in range(1, 32):
-        flag_copy(me, d).wait_send()
+    end_copies()
 
 
 def local(gases, pressure_bin, layer_mass, cos_zenith, surface_albedo, column_order, sunlit, absorption, scattering):
@@ -216,7 +283,7 @@
             pltpu.VMEM((G, C), BF16)] + state * 7 + [pltpu.VMEM((L, G, C), F32)] * 3 + [
             pltpu.VMEM((L + 1, 8, C), F32), pltpu.VMEM((4, 8, LANES), F32),
             pltpu.VMEM((L, C), F32), pltpu.VMEM((32, 1, 4), jnp.int32), pltpu.VMEM((8, C), F32),
-            pltpu.SemaphoreType.DMA((9,)), pltpu.SemaphoreType.DMA((32,)), pltpu.SemaphoreType.DMA((32,))],
+            pltpu.SemaphoreType.DMA((9,)), pltpu.SemaphoreType.DMA((33,)), pltpu.SemaphoreType.DMA((33,))],
         compiler_params=pltpu.CompilerParams(
             vmem_limit_bytes=60 * 1024 * 1024, collective_id=0, has_side_effects=True),
     )(gases, pressure_bin, layer_mass, cos_zenith, surface_albedo, column_order, sunlit.reshape(1, 4),

time: 19.2 us -> 17.3 us (0.901)
  the two profiles are of different devices: /device:TPU:6 before, /device:TPU:128 now
where the time goes in v3:
time: 17.3 us; the launch traced here: 17.2 us
  Pallas kernels  16.6 us (96%)
  local copies, waits for them, and re-layouts  0.63 us (4%)
    pallas_call x1, Pallas kernels, local(): pl.pallas_call(body, out_shape=pltpu.VMEM((L, C), F32), in_specs=[pl.Bloc...  16.6 us
    unnamed x1, local copies, waits for them, and re-layouts  0.63 us

profile of v3, /device:TPU:128, one launch (start us, length us, event | category | flops | bytes accessed | tf_op | source)
XLA Modules:
  0.0 17.2 jit_solution(16412205441305950713)
XLA Ops:
  0.0 16.6 %shard_map.91 = f32[32,512]{1,0:T(8,128)S(1)} custom-call(bf16[7,32,512]{2,1,0:T(8,128)(2,1)} %gas_hbm.1, s32[32,512]{1,0:T(8,128)} %bin_hbm.1, bf16[32,512]{1,0:T(8,128)(2,1)} %mass_hbm.1, bf16[512]{0:T(512)(128)(2,1)} %cos_hbm.1, bf16[512]{0:T(512)(128)(2,1)} %alb_hbm.1, s32[512]{0:T(512)} %order_hbm.1, s32[1,4]{1,0:T(1,128)} %bitcast.5, ...), custom_call_target="tpu_custom_call" | custom-call | tf_op jit(solution)/shard_map/pallas_call | solution.py:273
  16.6 0.6 %copy.11 = f32[32,512]{1,0:T(8,128)} copy(f32[32,512]{1,0:T(8,128)S(1)} %shard_map.91) | data formatting | bytes 131072

commit v4 on v3

--- a/solution.py
+++ b/solution.py
@@ -46,11 +46,13 @@
     hops = jnp.minimum(x, 2) + jnp.minimum(y, 2)
     direct = zl >= 2
     first = zh == 0
-    own_row = first | direct
+    corner = (zh == 1) & (q == 0) & jnp.logical_not(direct)
+    own_row = first | direct | corner
+    to_corner = jnp.logical_not(direct | corner)
     mine = zh * 16 + q
     moment = jnp.where(direct, jnp.where(first, 35 - 3 * zl - 3 * hops, 9 + 3 * zl - 3 * hops),
-                       jnp.where(first, 24 - 3 * hops, jnp.maximum(6 + 3 * zl - 3 * hops, 0))) // 2
-    expected = jnp.where(direct, 31, jnp.where(first, 15, 16))
+                       jnp.where(first, 24 - 5 * hops // 2, jnp.maximum(6 + 3 * zl - 3 * hops, 0))) // 2
+    expected = jnp.where(direct, 31, jnp.where(first | corner, 16, 17))
     barrier = pltpu.get_barrier_semaphore()
 
     def turn(d):
@@ -92,6 +94,11 @@
             src_ref=recv, dst_ref=recv, send_sem=ssem.at[32], recv_sem=rsem.at[32],
             device_id={"span": q * 2 + 1 - zh}, device_id_type=MESH)
 
+    def corner_copy():
+        return pltpu.make_async_remote_copy(
+            src_ref=sun_ref, dst_ref=recv.at[mine], send_sem=ssem.at[33], recv_sem=rsem.at[mine],
+            device_id={"span": 1}, device_id_type=MESH)
+
     def start_copy(plane, d):
         flag_copy(mine, plane, d).start()
 
@@ -107,6 +114,7 @@
             pl.semaphore_wait(barrier, expected)
             each(0, start_copy)
             pl.when(direct)(lambda: each(1, start_copy))
+            pl.when(to_corner)(lambda: corner_copy().start())
 
     def take_rows(when):
         @pl.when(when)
@@ -115,18 +123,21 @@
             each(0, take_row)
             each(1, take_row)
 
+    gives = first & jnp.logical_not(direct) & (q > 0)
+
     def hand_over():
-        take_rows(first & jnp.logical_not(direct))
-        pl.when(first & jnp.logical_not(direct))(lambda: table_copy().start())
+        take_rows(gives)
+        pl.when(gives)(lambda: table_copy().start())
 
     def finish_rows():
-        take_rows(direct)
+        take_rows(own_row & jnp.logical_not(gives))
         pl.when(jnp.logical_not(own_row))(lambda: table_copy().wait_recv())
 
     def end_copies():
         each(0, end_copy)
         pl.when(direct)(lambda: each(1, end_copy))
-        pl.when(first & jnp.logical_not(direct))(lambda: table_copy().wait_send())
+        pl.when(gives)(lambda: table_copy().wait_send())
+        pl.when(to_corner)(lambda: corner_copy().wait_send())
 
     send(moment == 0)
     for v in loads:
@@ -251,8 +262,9 @@
             return tuple(u)
 
         lax.fori_loop(0, L // 2, up, tuple(up0))
-
-    hand_over()
+        if half == 0:
+            hand_over()
+
     net = jnp.sum(acc[...], axis=1)
     heat[...] = (net[:L] - net[1:]) * (mu / mass_ref[...].astype(F32))
     finish_rows()
@@ -283,7 +295,7 @@
             pltpu.VMEM((G, C), BF16)] + state * 7 + [pltpu.VMEM((L, G, C), F32)] * 3 + [
             pltpu.VMEM((L + 1, 8, C), F32), pltpu.VMEM((4, 8, LANES), F32),
             pltpu.VMEM((L, C), F32), pltpu.VMEM((32, 1, 4), jnp.int32), pltpu.VMEM((8, C), F32),
-            pltpu.SemaphoreType.DMA((9,)), pltpu.SemaphoreType.DMA((33,)), pltpu.SemaphoreType.DMA((33,))],
+            pltpu.SemaphoreType.DMA((9,)), pltpu.SemaphoreType.DMA((34,)), pltpu.SemaphoreType.DMA((33,))],
         compiler_params=pltpu.CompilerParams(
             vmem_limit_bytes=60 * 1024 * 1024, collective_id=0, has_side_effects=True),
     )(gases, pressure_bin, layer_mass, cos_zenith, surface_albedo, column_order, sunlit.reshape(1, 4),

time: 17.3 us -> 16.6 us (0.960)
  the two profiles are of different devices: /device:TPU:128 before, /device:TPU:6 now
where the time goes in v4:
time: 16.6 us; the launch traced here: 16.5 us
  Pallas kernels  15.8 us (95%)
  local copies, waits for them, and re-layouts  0.63 us (4%)
    pallas_call x1, Pallas kernels, local(): pl.pallas_call(body, out_shape=pltpu.VMEM((L, C), F32), in_specs=[pl.Bloc...  15.8 us
    unnamed x1, local copies, waits for them, and re-layouts  0.63 us

profile of v4, /device:TPU:6, one launch (start us, length us, event | category | flops | bytes accessed | tf_op | source)
XLA Modules:
  0.0 16.5 jit_solution(10442151916312549621)
XLA Ops:
  0.0 15.8 %shard_map.91 = f32[32,512]{1,0:T(8,128)S(1)} custom-call(bf16[7,32,512]{2,1,0:T(8,128)(2,1)} %gas_hbm.1, s32[32,512]{1,0:T(8,128)} %bin_hbm.1, bf16[32,512]{1,0:T(8,128)(2,1)} %mass_hbm.1, bf16[512]{0:T(512)(128)(2,1)} %cos_hbm.1, bf16[512]{0:T(512)(128)(2,1)} %alb_hbm.1, s32[512]{0:T(512)} %order_hbm.1, s32[1,4]{1,0:T(1,128)} %bitcast.5, ...), custom_call_target="tpu_custom_call" | custom-call | tf_op jit(solution)/shard_map/pallas_call | solution.py:285
  15.8 0.6 %copy.11 = f32[32,512]{1,0:T(8,128)} copy(f32[32,512]{1,0:T(8,128)S(1)} %shard_map.91) | data formatting | bytes 131072

commit v5 on v4

--- a/solution.py
+++ b/solution.py
@@ -16,12 +16,9 @@
 G = 112
 C = 512
 TILES = G // 8
-INTERP = False
 
 
 def wide_row(ref, c, row, n):
-    if INTERP:
-        return jnp.broadcast_to(ref[c, pl.ds(row, 1), :], (n, LANES))
     return ref[c, pl.ds(row, n, stride=0), :]
 
 
@@ -51,7 +48,7 @@
     to_corner = jnp.logical_not(direct | corner)
     mine = zh * 16 + q
     moment = jnp.where(direct, jnp.where(first, 35 - 3 * zl - 3 * hops, 9 + 3 * zl - 3 * hops),
-                       jnp.where(first, 24 - 5 * hops // 2, jnp.maximum(6 + 3 * zl - 3 * hops, 0))) // 2
+                       jnp.where(first, 24 - 2 * hops, jnp.maximum(6 + 3 * zl - 3 * hops, 0))) // 2
     expected = jnp.where(direct, 31, jnp.where(first | corner, 16, 17))
     barrier = pltpu.get_barrier_semaphore()
 
@@ -71,17 +68,17 @@
     def signal(plane, d):
         pl.semaphore_signal(barrier, inc=1, device_id=device(plane, d), device_id_type=MESH)
 
-    @pl.when(own_row)
-    def _():
-        each(1, signal)
-        each(0, signal)
-
     loads = [pltpu.make_async_copy(src, dst, loc_sem.at[n]) for n, (src, dst) in enumerate((
         (abs_hbm, abs_ref), (sca_hbm, sca_ref), (gas_hbm, gas_ref), (bin_hbm, bin_ref), (cos_hbm, cos_ref),
         (alb_hbm, alb_ref), (order_hbm, order_ref), (mass_hbm, mass_ref)))]
     own = pltpu.make_async_copy(sun_ref, recv.at[mine], loc_sem.at[8])
     for v in loads:
         v.start()
+
+    @pl.when(own_row)
+    def _():
+        each(1, signal)
+        each(0, signal)
     pl.when(own_row)(lambda: own.start())
 
     def flag_copy(r, plane, d):
@@ -136,17 +133,17 @@
     def end_copies():
         each(0, end_copy)
         pl.when(direct)(lambda: each(1, end_copy))
-        pl.when(gives)(lambda: table_copy().wait_send())
         pl.when(to_corner)(lambda: corner_copy().wait_send())
 
     send(moment == 0)
-    for v in loads:
-        v.wait()
-
+    loads[2].wait()
+    loads[3].wait()
     for c in range(4):
         gas32[c] = gas_ref[:, :, cols(c)].reshape(GAS * L, LANES).astype(F32)
         bin32[c] = bin_ref[:, cols(c)].astype(F32)
     tab32[...] = jnp.zeros_like(tab32)
+    loads[0].wait()
+    loads[1].wait()
     for a in range(GAS):
         tab32[a * 64:a * 64 + 60, :G] = abs_ref[a].astype(F32)
     tab32[448:508, :G] = sca_ref[...].astype(F32) * 0.5
@@ -172,6 +169,8 @@
             h_ref[:, cs] = jnp.dot(lhs[:, 448:], sel, preferred_element_type=F32)
 
     optics(0, tau_a, h_a)
+    for v in loads[4:]:
+        v.wait()
     mu = cos_ref[...].astype(F32).reshape(1, C)
     rate = -LOG2E / mu
     alb = alb_ref[...].astype(F32).reshape(1, C)
@@ -234,7 +233,9 @@
     trow = (lax.rem(trow // 16, 2) * 16 + trow // 32).astype(F32).astype(BF16)
     order = order_ref[...].reshape(1, C)
     for c in range(4):
-        hot = (lax.broadcasted_iota(jnp.int32, (LANES, C), 0) + c * LANES == order).astype(F32).astype(BF16)
+        at = jnp.broadcast_to((order - c * LANES).astype(F32), (16, C)).astype(BF16)
+        at = jnp.concatenate([at] * 8, axis=0) == lax.broadcasted_iota(jnp.int32, (LANES, C), 0).astype(F32).astype(BF16)
+        hot = jnp.where(at, jnp.ones((LANES, C), BF16), jnp.zeros((LANES, C), BF16))
         jcol[:, cols(c)] = lax.dot_general(trow, hot, (((1,), (1,)), ((), ())), preferred_element_type=F32)
 
     for half in range(2):
@@ -253,7 +254,7 @@
             acc[L, :, cols(2 * half + j)] = sum(sums[j * TILES + 1:(j + 1) * TILES], sums[j * TILES])
 
         def up(k, u):
-            for l in (L - 1 - 2 * k, L - 2 - 2 * k):
+            for l in [L - 1 - n - 4 * k for n in range(4)]:
                 u = [ti_s[l, gs, cs] * u[n] + v_s[l, gs, cs] for n, (gs, cs) in enumerate(where)]
                 d = [p_s[l, gs, cs] * u[n] - u[n] for n, (gs, cs) in enumerate(where)]
                 for j in range(2):
@@ -261,12 +262,13 @@
                     acc[l, :, cs] = acc[l, :, cs] + sum(d[j * TILES + 1:(j + 1) * TILES], d[j * TILES])
             return tuple(u)
 
-        lax.fori_loop(0, L // 2, up, tuple(up0))
+        lax.fori_loop(0, L // 4, up, tuple(up0))
         if half == 0:
             hand_over()
 
     net = jnp.sum(acc[...], axis=1)
     heat[...] = (net[:L] - net[1:]) * (mu / mass_ref[...].astype(F32))
+    end_copies()
     finish_rows()
     flags = recv[...].reshape(32, 4)
     block = lax.broadcasted_iota(jnp.int32, (32, 4), 1) == me // 8
@@ -276,7 +278,7 @@
                   axis=0, keepdims=True)
     out_ref[...] = heat[...] * lit
 
-    end_copies()
+    pl.when(gives)(lambda: table_copy().wait_send())
 
 
 def local(gases, pressure_bin, layer_mass, cos_zenith, surface_albedo, column_order, sunlit, absorption, scattering):

time: 16.6 us -> 16.6 us (level)
  no operation moved by 1% of the time
where the time goes in v5:
time: 16.6 us; the launch traced here: 16.5 us
  Pallas kernels  15.9 us (96%)
  local copies, waits for them, and re-layouts  0.63 us (4%)
    pallas_call x1, Pallas kernels, local(): pl.pallas_call(body, out_shape=pltpu.VMEM((L, C), F32), in_specs=[pl.Bloc...  15.9 us
    unnamed x1, local copies, waits for them, and re-layouts  0.63 us

profile of v5, /device:TPU:6, one launch (start us, length us, event | category | flops | bytes accessed | tf_op | source)
XLA Modules:
  0.0 16.5 jit_solution(4403432882971539515)
XLA Ops:
  0.0 15.9 %shard_map.91 = f32[32,512]{1,0:T(8,128)S(1)} custom-call(bf16[7,32,512]{2,1,0:T(8,128)(2,1)} %gas_hbm.1, s32[32,512]{1,0:T(8,128)} %bin_hbm.1, bf16[32,512]{1,0:T(8,128)(2,1)} %mass_hbm.1, bf16[512]{0:T(512)(128)(2,1)} %cos_hbm.1, bf16[512]{0:T(512)(128)(2,1)} %alb_hbm.1, s32[512]{0:T(512)} %order_hbm.1, s32[1,4]{1,0:T(1,128)} %bitcast.5, ...), custom_call_target="tpu_custom_call" | custom-call | tf_op jit(solution)/shard_map/pallas_call | solution.py:287
  15.9 0.6 %copy.11 = f32[32,512]{1,0:T(8,128)} copy(f32[32,512]{1,0:T(8,128)S(1)} %shard_map.91) | data formatting | bytes 131072

commit v6 on v5

--- a/solution.py
+++ b/solution.py
@@ -47,8 +47,8 @@
     own_row = first | direct | corner
     to_corner = jnp.logical_not(direct | corner)
     mine = zh * 16 + q
-    moment = jnp.where(direct, jnp.where(first, 35 - 3 * zl - 3 * hops, 9 + 3 * zl - 3 * hops),
-                       jnp.where(first, 24 - 2 * hops, jnp.maximum(6 + 3 * zl - 3 * hops, 0))) // 2
+    moment = jnp.where(direct, jnp.where(first, 31 - 2 * zl - 3 * hops, 6 + 3 * zl - 3 * hops),
+                       jnp.where(first, 24 - 4 * zl - 2 * hops, jnp.maximum(6 + 3 * zl - 3 * hops, 0))) // 2
     expected = jnp.where(direct, 31, jnp.where(first | corner, 16, 17))
     barrier = pltpu.get_barrier_semaphore()
 

time: 16.6 us -> 16.6 us (level)
  no operation moved by 1% of the time
where the time goes in v6:
time: 16.6 us; the launch traced here: 16.5 us
  Pallas kernels  15.9 us (96%)
  local copies, waits for them, and re-layouts  0.63 us (4%)
    pallas_call x1, Pallas kernels, local(): pl.pallas_call(body, out_shape=pltpu.VMEM((L, C), F32), in_specs=[pl.Bloc...  15.9 us
    unnamed x1, local copies, waits for them, and re-layouts  0.63 us

profile of v6, /device:TPU:6, one launch (start us, length us, event | category | flops | bytes accessed | tf_op | source)
XLA Modules:
  0.0 16.5 jit_solution(10722495061325225708)
XLA Ops:
  0.0 15.9 %shard_map.91 = f32[32,512]{1,0:T(8,128)S(1)} custom-call(bf16[7,32,512]{2,1,0:T(8,128)(2,1)} %gas_hbm.1, s32[32,512]{1,0:T(8,128)} %bin_hbm.1, bf16[32,512]{1,0:T(8,128)(2,1)} %mass_hbm.1, bf16[512]{0:T(512)(128)(2,1)} %cos_hbm.1, bf16[512]{0:T(512)(128)(2,1)} %alb_hbm.1, s32[512]{0:T(512)} %order_hbm.1, s32[1,4]{1,0:T(1,128)} %bitcast.5, ...), custom_call_target="tpu_custom_call" | custom-call | tf_op jit(solution)/shard_map/pallas_call | solution.py:287
  15.9 0.6 %copy.11 = f32[32,512]{1,0:T(8,128)} copy(f32[32,512]{1,0:T(8,128)S(1)} %shard_map.91) | data formatting | bytes 131072

commit v7 on v6

--- a/solution.py
+++ b/solution.py
@@ -72,13 +72,14 @@
         (abs_hbm, abs_ref), (sca_hbm, sca_ref), (gas_hbm, gas_ref), (bin_hbm, bin_ref), (cos_hbm, cos_ref),
         (alb_hbm, alb_ref), (order_hbm, order_ref), (mass_hbm, mass_ref)))]
     own = pltpu.make_async_copy(sun_ref, recv.at[mine], loc_sem.at[8])
-    for v in loads:
-        v.start()
-
     @pl.when(own_row)
     def _():
         each(1, signal)
         each(0, signal)
+
+    for v in loads:
+        v.start()
+
     pl.when(own_row)(lambda: own.start())
 
     def flag_copy(r, plane, d):

time: 16.6 us -> 16.6 us (level)
  no operation moved by 1% of the time
where the time goes in v7:
time: 16.6 us; the launch traced here: 16.5 us
  Pallas kernels  15.8 us (95%)
  local copies, waits for them, and re-layouts  0.63 us (4%)
    pallas_call x1, Pallas kernels, local(): pl.pallas_call(body, out_shape=pltpu.VMEM((L, C), F32), in_specs=[pl.Bloc...  15.8 us
    unnamed x1, local copies, waits for them, and re-layouts  0.63 us

profile of v7, /device:TPU:6, one launch (start us, length us, event | category | flops | bytes accessed | tf_op | source)
XLA Modules:
  0.0 16.5 jit_solution(16600593531543992244)
XLA Ops:
  0.0 15.8 %shard_map.91 = f32[32,512]{1,0:T(8,128)S(1)} custom-call(bf16[7,32,512]{2,1,0:T(8,128)(2,1)} %gas_hbm.1, s32[32,512]{1,0:T(8,128)} %bin_hbm.1, bf16[32,512]{1,0:T(8,128)(2,1)} %mass_hbm.1, bf16[512]{0:T(512)(128)(2,1)} %cos_hbm.1, bf16[512]{0:T(512)(128)(2,1)} %alb_hbm.1, s32[512]{0:T(512)} %order_hbm.1, s32[1,4]{1,0:T(1,128)} %bitcast.5, ...), custom_call_target="tpu_custom_call" | custom-call | tf_op jit(solution)/shard_map/pallas_call | solution.py:288
  15.8 0.6 %copy.11 = f32[32,512]{1,0:T(8,128)} copy(f32[32,512]{1,0:T(8,128)S(1)} %shard_map.91) | data formatting | bytes 131072
